TPU v7x, 256 devices: a whole 4x4x8 slice. The times are simulated.
256 devices in a mesh: samp: 8 (over x, core), var: 32 (over z, y).
Axes of the slice: x: 4, y: 4, z: 8, core: 2. Of those that a mesh axis runs over, the one named last changes fastest.
Arguments:
- phenotype: bfloat16 [65536, 256], P(('samp', 'var')), may hold values from -1500 to 1500
- inverse_blocks: float32 [256, 256, 256], P(('samp', 'var')), may hold values from -1 to 2, as said below
- bin_sizes: int32 [8, 32], P('samp', 'var'), may hold values from 128 to 256, as said below
- slot_of: int32 [49152], P('samp'), may hold values from 0 to 8191, as said below
- dosages: bfloat16 [49152, 32768], P('samp', 'var'), may hold values from 0 to 2
Outputs:
- z_scores: float32 [32768, 256], P('var', 'samp')
Inputs may be any that keep to these rules, and one draw needn't show every extreme that they name: `bin_sizes`: within each row (one sample shard) the sizes sum to 192 times the row's length, and at least one bin is full. `slot_of`: within each sample shard the samples occupy exactly the live slots: slot v * 256 + r with r < bin_sizes of bin v, each once. `inverse_blocks`: each block is symmetric positive definite.
All inputs are finite; a program needn't handle non-finite values.
Results may differ from a plain program's by a relative error of at most 0.0041.
Values may be sent and summed in bfloat16 or wider, within the bound.
A program may use at most 128 MiB of HBM per device.

v0:
```python
import jax
import jax.numpy as jnp
from jax import lax
from jax.sharding import Mesh
from jax.sharding import PartitionSpec as P

SAMP_VAR = ("samp_0", "samp_1", "var_0", "var_1")
VAR = ("var_0", "var_1")
SAMP = ("samp_0", "samp_1")


epsilon = 1e-06


def one_axis_at_a_time(value, axes):
    for axis in axes:
        value = lax.psum(value, axis)
    return value


def gather_axes(value, axes, dim):
    if not axes:
        return value
    nearer = lax.all_gather(value, axes[-1], axis=dim, tiled=True)
    return gather_axes(nearer, axes[:-1], dim)


def in_blocks(value, dim, peers):
    before, after = (value.shape[:dim], value.shape[dim + 1 :])
    return jnp.moveaxis(value.reshape(*before, peers, -1, *after), dim, 0)


def sent_and_summed(value, axis, dim):
    peers = lax.axis_size(axis)
    pieces = lax.all_to_all(in_blocks(value, dim, peers), axis, 0, 0, tiled=True)
    return jnp.sum(pieces.astype(jnp.float32), axis=0)


def copy_for_each(value, axis):
    peers = lax.axis_size(axis)
    return lax.all_to_all(
        jnp.broadcast_to(value[None], (peers, *value.shape)), axis, 0, 0, tiled=True
    )


def taken_together(value, axis):
    return copy_for_each(value, axis).sum(axis=0)


def local(phenotype, inverse_blocks, bin_sizes, slot_of, dosages):
    bin_width = inverse_blocks.shape[1]
    position = jnp.arange(bin_width, dtype=jnp.int32)
    live_mask = (position < bin_sizes.reshape(())).astype(jnp.float32)[:, None]
    masked_pheno = phenotype.astype(jnp.float32) * live_mask
    whitened = (
        jnp.dot(
            inverse_blocks[0],
            masked_pheno,
            precision=lax.Precision.HIGHEST,
            preferred_element_type=jnp.float32,
        )
        * live_mask
    )
    trait_scale = one_axis_at_a_time(jnp.sum(masked_pheno * whitened, axis=0), SAMP_VAR)
    white_rows = whitened.astype(jnp.bfloat16)
    slot_weight = jnp.diagonal(inverse_blocks[0]).astype(jnp.bfloat16)
    gathered, weights_all = (gather_axes(white_rows, VAR, 0), gather_axes(slot_weight, VAR, 0))
    picked = jnp.take(gathered, slot_of, axis=0)
    score_part = lax.dot_general(
        dosages, picked, (((0,), (0,)), ((), ())), preferred_element_type=jnp.float32
    )
    sample_weight = jnp.take(weights_all, slot_of).astype(jnp.float32)
    variance = jnp.dot(
        sample_weight, dosages.astype(jnp.float32) ** 2, precision=lax.Precision.HIGHEST
    )
    trait_count = phenotype.shape[1] // lax.axis_size(SAMP)
    trait_start = lax.axis_index(SAMP) * trait_count
    score_share = sent_and_summed(score_part.astype(jnp.bfloat16), SAMP, 1)
    variance_all = taken_together(variance, SAMP)
    scale_share = lax.dynamic_slice_in_dim(trait_scale, trait_start, trait_count, 0)
    sample_count = slot_of.shape[0] * lax.axis_size(SAMP)
    return score_share / jnp.sqrt(
        variance_all[:, None] * scale_share[None, :] / sample_count + epsilon
    )


def solution(mesh):
    split = Mesh(mesh.devices.reshape(4, 2, 8, 4), ("samp_0", "samp_1", "var_0", "var_1"))
    in_specs = (P(SAMP_VAR, None), P(SAMP_VAR, None, None), P(SAMP, VAR), P(SAMP), P(SAMP, VAR))
    out_specs = P(VAR, SAMP)
    return jax.shard_map(local, mesh=split, in_specs=in_specs, out_specs=out_specs, check_vma=False)
```

profile of v0, /device:TPU:8, one launch (start us, length us, event | category | flops | bytes accessed | tf_op | source)
XLA Modules:
  0.0 200.2 jit_solution(13679015611097144882)
XLA Ops:
  6.5 0.0 copy-start
  6.5 0.0 all-gather.3.cloned.1.call-start
  7.2 0.3 copy-done
  7.5 1.5 multiply_reduce_fusion
  9.0 14.4 %all_gather.12 = bf16[1024,256]{1,0:T(8,128)(2,1)} all-gather(bf16[256,256]{1,0:T(8,128)(2,1)S(1)} %get-tuple-element.8), channel_id=1, replica_groups=mesh['samp_0'=4,'samp_1'=2,'var_0'=8,'var_1'=4] {'var_1'}, dimensions={0}, use_global_device_ids=true | all-gather | bytes 655360 | tf_op jit(solution)/shard_map/all_gather | solution.py:24
  23.4 0.0 all-gather.3.cloned.1.call-update
  23.4 2.3 %gather_fusion.1 = bf16[256]{0:T(256)(128)(2,1)S(1)} fusion(f32[256,256]{1,0:T(8,128)S(1)} %bitcast.20, s32[256]{0:T(256)S(1)} %bitcast.21), kind=kCustom, calls=%fused_computation.1 | custom fusion | bytes 3072 | tf_op jit(solution)/shard_map/jit(diagonal)/cond/branch_0_fun/gather | solution.py:66
  25.8 8.5 %all-gather = bf16[4,1,256]{2,1,0:T(2,128)(2,1)S(1)} all-gather(bf16[1,1,256]{2,1,0:T(2,128)(2,1)S(1)} %reshape.50), channel_id=1, replica_groups=mesh['samp_0'=4,'samp_1'=2,'var_0'=8,'var_1'=4] {'var_1'}, dimensions={0}, use_global_device_ids=true | all-gather | bytes 2560 | tf_op jit(solution)/shard_map/all_gather | solution.py:24
  34.4 24.0 %all_gather.15 = bf16[8192]{0:T(1024)(128)(2,1)S(1)} all-gather(bf16[1024]{0:T(1024)(128)(2,1)S(1)} %bitcast.24), channel_id=1, replica_groups=mesh['samp_0'=4,'samp_1'=2,'var_0'=8,'var_1'=4] {'var_0'}, dimensions={0}, use_global_device_ids=true | all-gather | bytes 18432 | tf_op jit(solution)/shard_map/all_gather | solution.py:24
  58.4 0.7 fusion.12
  59.1 0.0 copy-start.1
  59.1 38.2 %gather_fusion.2 = bf16[6144]{0:T(1024)(128)(2,1)S(1)} fusion(bf16[8192]{0:T(1024)(128)(2,1)S(1)} %all_gather.15, s32[6144]{0:T(1024)S(1)} %fusion.12), kind=kCustom, calls=%fused_computation.2 | custom fusion | bytes 49152 | tf_op jit(solution)/shard_map/jit(_take)/gather | solution.py:72
  97.3 0.0 copy-done.1
  97.4 12.3 %fusion = f32[1,1024]{1,0:T(1,128)S(1)} fusion(bf16[6144,1]{0,1:T(2,128)(2,1)S(1)} %reshape.52, bf16[6144,1024]{1,0:T(8,128)(2,1)} %param.9), kind=kOutput, calls=%fused_computation.3 | convolution fusion | flops 88080384 | bytes 12599296 | tf_op jit(solution)/shard_map/dot_general | solution.py:73
  109.7 0.6 broadcast_in_dim.35
  110.3 4.3 %all-to-all-start.1 = ((f32[8,1,1024]{2,1,0:T(1,128)}), f32[8,1,1024]{2,1,0:T(1,128)S(1)}, u32[]{:S(2)}, u32[]{:S(2)}) async-start(f32[8,1,1024]{2,1,0:T(1,128)} %broadcast_in_dim.35), calls=%async_computation.1 | async-start | bytes 65536 | tf_op jit(solution)/shard_map/all_to_all | solution.py:41
  114.6 0.0 all-gather.3.cloned.1.call-done
  114.6 22.1 %gather_fusion = bf16[6144,256]{1,0:T(8,128)(2,1)S(1)} fusion(bf16[8192,256]{1,0:T(8,128)(2,1)} %all-gather.3.cloned.1.call-done, s32[6144]{0:T(1024)S(1)} %fusion.12), kind=kCustom, calls=%fused_computation | custom fusion | bytes 6316032 | tf_op jit(solution)/shard_map/jit(_take)/gather | solution.py:68
  136.7 9.7 %fusion.7 = bf16[256,1024]{1,0:T(8,128)(2,1)} fusion(bf16[6144,1024]{1,0:T(8,128)(2,1)} %param.9, bf16[6144,256]{1,0:T(8,128)(2,1)S(1)} %gather_fusion, pred[6144]{0:T(1024)(128)(4,1)S(1)} %get-tuple-element.6), kind=kOutput, calls=%fused_computation.10 | convolution fusion | flops 3223060480 | bytes 16259072 | tf_op jit(solution)/shard_map/dot_general | solution.py:69
  146.4 0.0 all-to-all-done.1
  146.4 4.8 %all-to-all-start = ((bf16[8,1024,32]{1,2,0:T(8,128)(2,1)}), bf16[8,1024,32]{1,2,0:T(8,128)(2,1)S(1)}, u32[]{:S(2)}, u32[]{:S(2)}) async-start(bf16[8,1024,32]{1,2,0:T(8,128)(2,1)} %bitcast.22), calls=%async_computation | async-start | bytes 1048576 | tf_op jit(solution)/shard_map/all_to_all | solution.py:35
  151.2 12.6 %psum.28 = f32[256]{0:T(256)S(1)} all-reduce(f32[256]{0:T(256)S(1)} %get-tuple-element.7), channel_id=1, replica_groups=mesh['samp_0'=4,'samp_1'=2,'var_0'=8,'var_1'=4] {'samp_0'}, use_global_device_ids=true, to_apply=%region_3.0 | all-reduce | flops 256 | bytes 2048 | tf_op jit(solution)/shard_map/psum | solution.py:17
  163.8 2.4 %psum.29 = f32[256]{0:T(256)S(1)} all-reduce(f32[256]{0:T(256)S(1)} %psum.28), channel_id=1, replica_groups=mesh['samp_0'=4,'samp_1'=2,'var_0'=8,'var_1'=4] {'samp_1'}, use_global_device_ids=true, to_apply=%region_4.0 | all-reduce | flops 256 | bytes 2048 | tf_op jit(solution)/shard_map/psum | solution.py:17
  166.2 15.4 %psum.30 = f32[256]{0:T(256)S(1)} all-reduce(f32[256]{0:T(256)S(1)} %psum.29), channel_id=1, replica_groups=mesh['samp_0'=4,'samp_1'=2,'var_0'=8,'var_1'=4] {'var_0'}, use_global_device_ids=true, to_apply=%region_5.6 | all-reduce | flops 256 | bytes 2048 | tf_op jit(solution)/shard_map/psum | solution.py:17
  181.6 10.8 %psum.31 = f32[256]{0:T(256)S(1)} all-reduce(f32[256]{0:T(256)S(1)} %psum.30), channel_id=1, replica_groups=mesh['samp_0'=4,'samp_1'=2,'var_0'=8,'var_1'=4] {'var_1'}, use_global_device_ids=true, to_apply=%region_6.7 | all-reduce | flops 256 | bytes 2048 | tf_op jit(solution)/shard_map/psum | solution.py:17
  192.4 0.1 dynamic_slice.3
  192.5 0.0 all-to-all-done
  192.5 0.1 convert_reduce_fusion
  192.6 0.8 rsqrt_multiply_fusion
  (8 shorter events, 0.1 us)
Async XLA Ops:
  6.5 1.0 copy-start
  6.5 108.1 %all-gather.3.cloned.1.call-start = ((), (), s32[]{:S(2)}) async-start(), calls=%async_computation.2 | async-start | bytes 4718592 | tf_op jit(solution)/shard_map/all_gather | solution.py:24
  59.1 38.2 %copy-start.1 = (s32[6144]{0:T(1024)S(1)}, s32[6144]{0:T(1024)}, u32[]{:S(2)}) copy-start(s32[6144]{0:T(1024)} %param.8) | copy-start | bytes 73732
  110.3 36.1 %all-to-all-start.1 = ((f32[8,1,1024]{2,1,0:T(1,128)}), f32[8,1,1024]{2,1,0:T(1,128)S(1)}, u32[]{:S(2)}, u32[]{:S(2)}) async-start(f32[8,1,1024]{2,1,0:T(1,128)} %broadcast_in_dim.35), calls=%async_computation.1 | async-start | bytes 65536 | tf_op jit(solution)/shard_map/all_to_all | solution.py:41
  146.4 46.1 %all-to-all-start = ((bf16[8,1024,32]{1,2,0:T(8,128)(2,1)}), bf16[8,1024,32]{1,2,0:T(8,128)(2,1)S(1)}, u32[]{:S(2)}, u32[]{:S(2)}) async-start(bf16[8,1024,32]{1,2,0:T(8,128)(2,1)} %bitcast.22), calls=%async_computation | async-start | bytes 1048576 | tf_op jit(solution)/shard_map/all_to_all | solution.py:35
Sparse Core Ops, SparseCore 0:
  23.5 57.5 all-gather.2
where the time goes:
time: 201 us; the launch traced here: 200 us
  blocking collectives  88.2 us (44%)
  local copies, waits for them, and re-layouts  63.6 us (32%)
  matrix products  23.4 us (12%)
  between operations  14.2 us (7%)
  starting transfers between devices  9.07 us (5%)
    all_gather x3, blocking collectives, gather_axes(): nearer = lax.all_gather(value, axes[-1], axis=dim, tiled=True)  47 us
    psum x4, blocking collectives, one_axis_at_a_time(): value = lax.psum(value, axis)  41.3 us
    gather x1, local copies, waits for them, and re-layouts, local(): sample_weight = jnp.take(weights_all, slot_of).astype(jnp.float32)  38.2 us
    gather x1, local copies, waits for them, and re-layouts, local(): picked = jnp.take(gathered, slot_of, axis=0)  22.1 us
    dot_general x1, matrix products, local(): jnp.dot(sample_weight, dosages.astype(jnp.float32) ** 2, precision=lax.Pr...  12.3 us
    dot_general x1, matrix products, local(): lax.dot_general(dosages, picked, (((0,), (0,)), ((), ())), preferred_elem...  9.66 us
    all_to_all x1, starting transfers between devices, sent_and_summed(): lax.all_to_all(in_blocks(value, dim, peers), axis, 0, 0, tiled=True)  4.78 us
    all_to_all x1, starting transfers between devices, copy_for_each(): lax.all_to_all(jnp.broadcast_to(value[None], (peers, *value.shape)), axis...  4.29 us
  transfers between devices with their start and end apart: 3, of which 0 were waited for; matrix products, arithmetic and copies ran while one was open for 43% of the time, Pallas kernels for 0%

commit v1 on v0

v1 whole, which is shorter than its diff:
```python
import heapq

import jax
import jax.numpy as jnp
from jax import lax
from jax.experimental import pallas as pl
from jax.experimental.pallas import tpu as pltpu
from jax.sharding import Mesh
from jax.sharding import PartitionSpec as P

MESH = pl.DeviceIdType.MESH
X, CORE, Z, Y = "samp_0", "samp_1", "var_0", "var_1"
NX, NZ, NY = 4, 8, 4
NBINS = NZ * NY
B = 256
T = 256
N = 6144
M = 1024
N_ALL = 49152
EPS = 1e-6
MSG = T + 16
TS = 128 * 10

PARTS = {"A": (0, 160), "B": (160, MSG - 160)}
HOPS_Z = [0, 1, -1, 2, -2, 3, -3, 4]
HOPS_Y = [0, 1, -1, 2]


def slot(a, b):
    return HOPS_Z.index(a) * NY + HOPS_Y.index(b)


def forwards(part, a, b):
    along_z, along_y = [], []
    if 0 <= a < 4:
        along_z.append((Z, 1, a + 1, b))
    if -3 < a <= 0:
        along_z.append((Z, -1, a - 1, b))
    if 0 <= b < 2:
        along_y.append((Y, 1, a, b + 1))
    if -1 < b <= 0:
        along_y.append((Y, -1, a, b - 1))
    if part == "A":
        return (along_z if b == 0 else []) + along_y
    return along_z + (along_y if a == 0 else [])


def gather_order(rate, latency, single):
    queue = {(ax, d): [] for ax in (Z, Y) for d in (1, -1)}
    arriving, order, step, now, count = [], [], 0.02, 0.0, 0

    def send(p, a, b):
        for ax, d, a2, b2 in forwards(p, a, b):
            queue[(ax, d)].append([PARTS[p][1] * 0.512, p, a2, b2])

    for p in PARTS:
        order.append((0.0, p, 0, 0))
        send(p, 0, 0)
    while arriving or any(queue.values()):
        now += step
        for ax in (Z, Y):
            active = [d for d in (1, -1) if queue[(ax, d)]]
            for d in active:
                left = (rate / 2 if len(active) == 2 else single) * step
                while left > 0 and queue[(ax, d)]:
                    head = queue[(ax, d)][0]
                    used = min(left, head[0])
                    head[0] -= used
                    left -= used
                    if head[0] <= 1e-9:
                        queue[(ax, d)].pop(0)
                        count += 1
                        heapq.heappush(arriving, (now + latency, count, *head[1:]))
        while arriving and arriving[0][0] <= now:
            when, _, p, a, b = heapq.heappop(arriving)
            order.append((when, p, a, b))
            send(p, a, b)
    return order


GATHER = gather_order(90.0, 3.0, 75.0)
LOADS = 12
ROWS = N // LOADS
GROUP = 32
COST = dict(split=0.6, pick=0.055, multiply=0.22)


def prepare_kernel(pheno_ref, inv_ref, size_ref, slot_ref, msg_ref, sample_ref):
    size = size_ref[0, 0]
    row = lax.broadcasted_iota(jnp.int32, (B, T), 0)
    col = lax.broadcasted_iota(jnp.int32, (B, T), 1)
    omega = inv_ref[0]
    masked = jnp.where(row < size, pheno_ref[...].astype(jnp.float32), 0.0)
    masked_16 = masked.astype(jnp.bfloat16)
    rest, total = omega, None
    for _ in range(3):
        piece = rest.astype(jnp.bfloat16)
        rest = rest - piece.astype(jnp.float32)
        term = jnp.dot(piece, masked_16, preferred_element_type=jnp.float32)
        total = term if total is None else total + term
    white = jnp.where(row < size, total, 0.0)
    scale = jnp.sum(masked * white, axis=0, keepdims=True)
    weight = jnp.sum(jnp.where(row == col, omega, 0.0), axis=0, keepdims=True)
    weight = jnp.where(col[:1] < size, weight, 0.0)
    turned = white.T
    for c in range(2):
        for x in range(4):
            trait = (2 * x + c) * 32
            at = c * 128 + x * 32
            msg_ref[at : at + 32, :] = turned[trait : trait + 32, :].astype(jnp.bfloat16)
    s0 = scale.astype(jnp.bfloat16).astype(jnp.float32)
    s1 = (scale - s0).astype(jnp.bfloat16).astype(jnp.float32)
    s2 = scale - s0 - s1
    line = lax.broadcasted_iota(jnp.int32, (16, T), 0)
    extra = jnp.where(line == 0, weight, jnp.where(line == 1, s0, jnp.where(line == 2, s1, jnp.where(line == 3, s2, 0.0))))
    msg_ref[T:MSG, :] = extra.astype(jnp.bfloat16)

    found = jnp.zeros((128, 128), jnp.float32)
    chunk = 1024
    for k in range(N // chunk):
        slots = slot_ref[:, k * chunk : (k + 1) * chunk]
        high, low = slots // 128, slots % 128
        at = lax.broadcasted_iota(jnp.int32, (128, chunk), 0)
        sample = lax.broadcasted_iota(jnp.int32, (128, chunk), 1) + k * chunk
        digit = jnp.where(at < 64, sample // 128, sample % 128).astype(jnp.float32)
        left = jnp.where(at % 64 == high, digit, 0.0).astype(jnp.bfloat16)
        right = jnp.where(at == low, 1.0, 0.0).astype(jnp.bfloat16)
        found += lax.dot_general(left, right, (((1,), (1,)), ((), ())), preferred_element_type=jnp.float32)
    sample_ref[...] = (found[:64] * 128.0 + found[64:]).astype(jnp.int32)


def prepare(phenotype, inverse_blocks, bin_sizes, slot_of):
    vmem = pl.BlockSpec(memory_space=pltpu.VMEM)
    return pl.pallas_call(
        prepare_kernel,
        name="prepare",
        out_shape=(jax.ShapeDtypeStruct((MSG, T), jnp.bfloat16), jax.ShapeDtypeStruct((64, 128), jnp.int32)),
        in_specs=[vmem, vmem, pl.BlockSpec(memory_space=pltpu.SMEM), vmem],
        out_specs=(vmem, vmem),
    )(phenotype, inverse_blocks, bin_sizes, slot_of.reshape(1, N))


def scores_kernel(
    sample_ref, msg_ref, dosage_ref, out_ref,
    split, ordered, got, acc, var_acc,
    half_out, half_in, part_out, part_in, small_out, small_in,
    send_sem, recv_sem, load_sem, own_sem, half_send, half_recv, part_send, part_recv, small_send, small_recv,
):
    x, core, z, y = (lax.axis_index(name) for name in (X, CORE, Z, Y))
    forward = 1 - 2 * core
    neighbour = {
        (Z, 1): (x, core, (z + forward + NZ) % NZ, y),
        (Z, -1): (x, core, (z - forward + NZ) % NZ, y),
        (Y, 1): (x, core, z, (y + forward + NY) % NY),
        (Y, -1): (x, core, z, (y - forward + NY) % NY),
    }
    sibling = (x, 1 - core, z, y)
    peers = {d: ((x + d) % NX, core, z, y) for d in (1, 2, 3)}
    partners = [*neighbour.values(), sibling, *peers.values()]

    loads = [
        pltpu.make_async_copy(
            dosage_ref.at[pl.ds(i * ROWS, ROWS)], ordered.at[pl.ds(i * ROWS, ROWS)], load_sem.at[i]
        )
        for i in range(LOADS)
    ]
    own = pltpu.make_async_copy(msg_ref, got.at[0], own_sem)
    own.start()
    for load in loads:
        load.start()

    barrier = pltpu.get_barrier_semaphore()
    for partner in partners:
        pl.semaphore_signal(barrier, inc=1, device_id=partner, device_id_type=MESH)
    acc[...] = jnp.zeros_like(acc)
    var_acc[...] = jnp.zeros_like(var_acc)
    own.wait()
    pl.semaphore_wait(barrier, len(partners))

    def remote(source, target, send, recv, device):
        return pltpu.make_async_remote_copy(
            src_ref=source, dst_ref=target, send_sem=send, recv_sem=recv, device_id=device, device_id_type=MESH
        )

    def part_of(p, a, b):
        first, count = PARTS[p]
        return got.at[slot(a, b), pl.ds(first, count)]

    part_index = {p: i for i, p in enumerate(PARTS)}
    sends = []

    def await_and_forward(p, a, b):
        if (a, b) != (0, 0):
            here = part_of(p, a, b)
            remote(here, here, send_sem.at[0], recv_sem.at[part_index[p], slot(a, b)], sibling).wait_recv()
        for ax, d, a2, b2 in forwards(p, a, b):
            copy = remote(
                part_of(p, a, b), part_of(p, a2, b2), send_sem.at[len(sends)],
                recv_sem.at[part_index[p], slot(a2, b2)], neighbour[(ax, d)],
            )
            copy.start()
            sends.append(copy)

    flat = split.reshape(N * 8, 128)

    def split_rows(i):
        loads[i].wait()

        @pl.loop(0, ROWS // 16)
        def _(g):
            row = pl.multiple_of(i * ROWS + g * 16, 16)
            value = ordered[pl.ds(row, 16), :].astype(jnp.float32)
            base = pl.multiple_of(row * 8, 128)
            for h in range(2):
                for j in range(8):
                    flat[pl.ds(base + h * 64 + j, 8, stride=8), :] = value[8 * h : 8 * h + 8, 128 * j : 128 * j + 128]

    def pick_rows(first, last):
        @pl.loop(first, last)
        def _(g):
            t = g // (B // GROUP)
            ia, ib = t // NY, t % NY
            a = (1 - 2 * ((ia + 1) % 2)) * ((ia + 1) // 2)
            b = (1 - 2 * ((ib + 1) % 2)) * ((ib + 1) // 2)
            origin = ((z - forward * a + NZ) % NZ) * NY + (y - forward * b + NY) % NY
            start = origin * B + (g % (B // GROUP)) * GROUP
            for q in range(GROUP // 16):
                rows = jnp.stack([split[sample_ref[start + q * 16 + u]] for u in range(16)], 0)
                turned = pltpu.einshape("kjl->jkl", rows).astype(jnp.bfloat16)
                at = pl.multiple_of(g * GROUP + q * 16, 16)
                for j in range(8):
                    ordered[pl.ds(at, 16), 128 * j : 128 * j + 128] = turned[j]

    def multiply(t):
        @pl.loop(0, M // 256)
        def _(n):
            columns = pl.ds(pl.multiple_of(n * 256, 256), 256)
            right = ordered[pl.ds(t * B, B), columns]
            acc[:, columns] += jnp.dot(got[t, :T, :], right, preferred_element_type=jnp.float32)
            var_acc[:, columns] += jnp.dot(got[t, T:, :], right * right, preferred_element_type=jnp.float32)

    clock = 0.0
    to_split = list(range(LOADS))
    picked, groups = 0, NBINS * B // GROUP
    seen, ready = {}, []

    def work(until):
        nonlocal clock, picked
        while clock < until:
            if to_split:
                split_rows(to_split.pop(0))
                clock += COST["split"]
            elif ready and (ready[0] + 1) * (B // GROUP) <= picked:
                multiply(ready.pop(0))
                clock += COST["multiply"]
            elif picked < groups:
                count = min(B // GROUP, groups - picked)
                pick_rows(picked, picked + count)
                picked += count
                clock += COST["pick"] * count
            else:
                return

    for when, p, a, b in GATHER:
        work(when)
        await_and_forward(p, a, b)
        seen[(a, b)] = seen.get((a, b), 0) + 1
        if seen[(a, b)] == len(PARTS):
            ready.append(slot(a, b))
            ready.sort()
    work(float("inf"))
    for copy in sends:
        copy.wait_send()

    scale = got[0, T + 1 : T + 4, :].astype(jnp.float32).sum(axis=0, keepdims=True)
    for t in range(1, NBINS):
        scale += got[t, T + 1 : T + 4, :].astype(jnp.float32).sum(axis=0, keepdims=True)
    small_out[0, :, :M] = var_acc[0:1, :]
    small_out[0, :, M:] = scale
    smalls = [remote(small_out.at[0], small_in.at[0], small_send.at[0], small_recv.at[0], sibling)]
    smalls[0].start()

    halves = {}
    for d in (2, 1, 3, 0):
        rows = pl.ds(pl.multiple_of((1 - core) * 128 + ((x + d) % NX) * 32, 32), 32)
        half_out[d] = acc[rows, :].astype(jnp.bfloat16)
        halves[d] = remote(half_out.at[d], half_in.at[d], half_send.at[d], half_recv.at[d], sibling)
        halves[d].start()

    smalls[0].wait()
    small_out[1] = small_out[0] + small_in[0]
    for d in (1, 2, 3):
        copy = remote(small_out.at[1], small_in.at[d], small_send.at[d], small_recv.at[d], peers[d])
        copy.start()
        smalls.append(copy)

    pieces = []
    for d in (2, 1, 3, 0):
        rows = pl.ds(pl.multiple_of(core * 128 + ((x + d) % NX) * 32, 32), 32)
        halves[d].wait()
        both = acc[rows, :] + half_in[d].astype(jnp.float32)
        if d == 0:
            total = both
        else:
            part_out[d - 1] = both.astype(jnp.bfloat16)
            copy = remote(part_out.at[d - 1], part_in.at[d - 1], part_send.at[d - 1], part_recv.at[d - 1], peers[d])
            copy.start()
            pieces.append(copy)
    for copy in smalls[1:]:
        copy.wait()
    small = small_out[1] + small_in[1] + small_in[2] + small_in[3]
    variance, scale = small[:, :M], small[:, M:]
    trait = (2 * x + core) * 32 + lax.broadcasted_iota(jnp.int32, (32, T), 0)
    lane = lax.broadcasted_iota(jnp.int32, (32, T), 1)
    share = jnp.sum(jnp.where(lane == trait, scale, 0.0), axis=1, keepdims=True)
    root = lax.rsqrt(variance * share / N_ALL + EPS)
    for copy in pieces:
        copy.wait()
    for d in range(3):
        total += part_in[d].astype(jnp.float32)
    out_ref[...] = total * root


def score(samples, message, dosages):
    vmem = pl.BlockSpec(memory_space=pltpu.VMEM)
    anywhere = pl.BlockSpec(memory_space=pl.ANY)
    dma = pltpu.SemaphoreType.DMA
    n_sends = sum(len(forwards(p, a, b)) for _, p, a, b in GATHER)
    return pl.pallas_call(
        scores_kernel,
        name="scores",
        out_shape=jax.ShapeDtypeStruct((32, M), jnp.float32),
        in_specs=[pl.BlockSpec(memory_space=pltpu.SMEM), anywhere, anywhere],
        out_specs=vmem,
        scratch_shapes=[
            pltpu.VMEM((N, 8, 128), jnp.float32),
            pltpu.VMEM((NBINS * B, M), jnp.bfloat16),
            pltpu.VMEM((NBINS, MSG, B), jnp.bfloat16),
            pltpu.VMEM((T, M), jnp.float32),
            pltpu.VMEM((16, M), jnp.float32),
            pltpu.VMEM((4, 32, M), jnp.bfloat16),
            pltpu.VMEM((4, 32, M), jnp.bfloat16),
            pltpu.VMEM((3, 32, M), jnp.bfloat16),
            pltpu.VMEM((3, 32, M), jnp.bfloat16),
            pltpu.VMEM((2, 1, TS), jnp.float32),
            pltpu.VMEM((4, 1, TS), jnp.float32),
            dma((n_sends,)), dma((2, NBINS)), dma((LOADS,)), dma,
            dma((4,)), dma((4,)), dma((3,)), dma((3,)), dma((4,)), dma((4,)),
        ],
        compiler_params=pltpu.CompilerParams(
            collective_id=0, has_side_effects=True, vmem_limit_bytes=58 << 20
        ),
    )(samples, message, dosages)


def local(phenotype, inverse_blocks, bin_sizes, slot_of, dosages):
    message, samples = prepare(phenotype, inverse_blocks, bin_sizes, slot_of)
    return score(samples.reshape(NBINS * B), message, dosages).T


def solution(mesh):
    split = Mesh(mesh.devices.reshape(NX, 2, NZ, NY), (X, CORE, Z, Y))
    samp, var, both = (X, CORE), (Z, Y), (X, CORE, Z, Y)
    in_specs = (P(both, None), P(both, None, None), P(samp, var), P(samp), P(samp, var))
    return jax.shard_map(local, mesh=split, in_specs=in_specs, out_specs=P(var, samp), check_vma=False)
```

time: 201 us -> 85 us (0.42)
  the two profiles are of different devices: /device:TPU:8 before, /device:TPU:1 now
where the time goes in v1:
time: 85 us; the launch traced here: 84.8 us
  Pallas kernels  82.5 us (97%)
  local copies, waits for them, and re-layouts  1.57 us (2%)
    pallas_call x1, Pallas kernels, score(): pl.pallas_call(scores_kernel, name='scores', out_shape=jax.ShapeDtypeStru...  80.1 us
    pallas_call x1, Pallas kernels, prepare(): pl.pallas_call(prepare_kernel, name='prepare', out_shape=(jax.ShapeDtypeS...  2.4 us

profile of v1, /device:TPU:1, one launch (start us, length us, event | category | flops | bytes accessed | tf_op | source)
XLA Modules:
  0.0 84.8 jit_solution(10372654242831181396)
XLA Ops:
  0.7 2.4 %prepare.1 = (bf16[272,256]{1,0:T(8,128)(2,1)}, s32[64,128]{1,0:T(8,128)}) custom-call(bf16[256,256]{1,0:T(8,128)(2,1)} %pheno_ref.1, f32[1,256,256]{2,1,0:T(8,128)} %inv_ref.1, s32[1,1]{1,0:T(1,128)S(6)} %copy.7.size_ref, s32[1,6144]{1,0:T(1,128)} %bitcast.5), custom_call_target="tpu_custom_call" | custom-call | tf_op jit(solution)/shard_map/prepare/pallas_call | solution.py:134
  3.0 80.1 %scores.1 = f32[32,1024]{1,0:T(8,128)} custom-call(s32[8192]{0:T(1024)} %bitcast.4, bf16[272,256]{1,0:T(8,128)(2,1)} %get-tuple-element.8.msg_ref, bf16[6144,1024]{1,0:T(8,128)(2,1)} %dosage_ref.1), custom_call_target="tpu_custom_call" | custom-call | tf_op jit(solution)/shard_map/scores/pallas_call | solution.py:329
  83.2 1.6 %copy.8 = f32[1024,32]{0,1:T(8,128)} copy(f32[1024,32]{0,1:T(8,128)} %bitcast.3) | data formatting | bytes 262144

commit v2 on v1

--- a/solution.py
+++ b/solution.py
@@ -78,18 +78,46 @@
     return order
 
 
-GATHER = gather_order(90.0, 3.0, 75.0)
-LOADS = 12
+GATHER = gather_order(90.0, 4.0, 75.0)
+LOADS = 24
 ROWS = N // LOADS
-GROUP = 32
-COST = dict(split=0.6, pick=0.055, multiply=0.22)
-
-
-def prepare_kernel(pheno_ref, inv_ref, size_ref, slot_ref, msg_ref, sample_ref):
+GROUP = 64
+PACE, LEAD = 0.8, 0.0
+LOADED = (1.5, 0.3)
+COST = dict(split=0.3, pick=0.3, multiply=0.58, forward=0.05)
+
+
+def invert_kernel(slot_ref, sample_ref):
+    found = jnp.zeros((128, 128), jnp.float32)
+    chunk = 1024
+    for k in range(N // chunk):
+        slots = slot_ref[:, k * chunk : (k + 1) * chunk]
+        high, low = slots // 128, slots % 128
+        at = lax.broadcasted_iota(jnp.int32, (128, chunk), 0)
+        sample = lax.broadcasted_iota(jnp.int32, (128, chunk), 1) + k * chunk
+        digit = jnp.where(at < 64, sample // 128, sample % 128).astype(jnp.float32)
+        left = jnp.where(at % 64 == high, digit, 0.0).astype(jnp.bfloat16)
+        right = jnp.where(at == low, 1.0, 0.0).astype(jnp.bfloat16)
+        found += lax.dot_general(left, right, (((1,), (1,)), ((), ())), preferred_element_type=jnp.float32)
+    sample_ref[...] = (found[:64] * 128.0 + found[64:]).astype(jnp.int32)
+
+
+def invert(slot_of):
+    vmem = pl.BlockSpec(memory_space=pltpu.VMEM)
+    return pl.pallas_call(
+        invert_kernel,
+        name="invert",
+        out_shape=jax.ShapeDtypeStruct((64, 128), jnp.int32),
+        in_specs=[vmem],
+        out_specs=vmem,
+    )(slot_of.reshape(1, N))
+
+
+def whiten(pheno_ref, omega_ref, size_ref, message_ref):
     size = size_ref[0, 0]
     row = lax.broadcasted_iota(jnp.int32, (B, T), 0)
     col = lax.broadcasted_iota(jnp.int32, (B, T), 1)
-    omega = inv_ref[0]
+    omega = omega_ref[0]
     masked = jnp.where(row < size, pheno_ref[...].astype(jnp.float32), 0.0)
     masked_16 = masked.astype(jnp.bfloat16)
     rest, total = omega, None
@@ -107,42 +135,18 @@
         for x in range(4):
             trait = (2 * x + c) * 32
             at = c * 128 + x * 32
-            msg_ref[at : at + 32, :] = turned[trait : trait + 32, :].astype(jnp.bfloat16)
+            message_ref[at : at + 32, :] = turned[trait : trait + 32, :].astype(jnp.bfloat16)
     s0 = scale.astype(jnp.bfloat16).astype(jnp.float32)
     s1 = (scale - s0).astype(jnp.bfloat16).astype(jnp.float32)
     s2 = scale - s0 - s1
     line = lax.broadcasted_iota(jnp.int32, (16, T), 0)
     extra = jnp.where(line == 0, weight, jnp.where(line == 1, s0, jnp.where(line == 2, s1, jnp.where(line == 3, s2, 0.0))))
-    msg_ref[T:MSG, :] = extra.astype(jnp.bfloat16)
-
-    found = jnp.zeros((128, 128), jnp.float32)
-    chunk = 1024
-    for k in range(N // chunk):
-        slots = slot_ref[:, k * chunk : (k + 1) * chunk]
-        high, low = slots // 128, slots % 128
-        at = lax.broadcasted_iota(jnp.int32, (128, chunk), 0)
-        sample = lax.broadcasted_iota(jnp.int32, (128, chunk), 1) + k * chunk
-        digit = jnp.where(at < 64, sample // 128, sample % 128).astype(jnp.float32)
-        left = jnp.where(at % 64 == high, digit, 0.0).astype(jnp.bfloat16)
-        right = jnp.where(at == low, 1.0, 0.0).astype(jnp.bfloat16)
-        found += lax.dot_general(left, right, (((1,), (1,)), ((), ())), preferred_element_type=jnp.float32)
-    sample_ref[...] = (found[:64] * 128.0 + found[64:]).astype(jnp.int32)
-
-
-def prepare(phenotype, inverse_blocks, bin_sizes, slot_of):
-    vmem = pl.BlockSpec(memory_space=pltpu.VMEM)
-    return pl.pallas_call(
-        prepare_kernel,
-        name="prepare",
-        out_shape=(jax.ShapeDtypeStruct((MSG, T), jnp.bfloat16), jax.ShapeDtypeStruct((64, 128), jnp.int32)),
-        in_specs=[vmem, vmem, pl.BlockSpec(memory_space=pltpu.SMEM), vmem],
-        out_specs=(vmem, vmem),
-    )(phenotype, inverse_blocks, bin_sizes, slot_of.reshape(1, N))
+    message_ref[T:MSG, :] = extra.astype(jnp.bfloat16)
 
 
 def scores_kernel(
-    sample_ref, msg_ref, dosage_ref, out_ref,
-    split, ordered, got, acc, var_acc,
+    size_ref, sample_hbm, pheno_hbm, omega_hbm, dosage_ref, out_ref,
+    sample_ref, pheno_ref, omega_ref, split, ordered, got, acc, var_acc, scale_acc,
     half_out, half_in, part_out, part_in, small_out, small_in,
     send_sem, recv_sem, load_sem, own_sem, half_send, half_recv, part_send, part_recv, small_send, small_recv,
 ):
@@ -164,17 +168,20 @@
         )
         for i in range(LOADS)
     ]
-    own = pltpu.make_async_copy(msg_ref, got.at[0], own_sem)
-    own.start()
-    for load in loads:
-        load.start()
-
+    own = [
+        pltpu.make_async_copy(source, target, own_sem.at[i])
+        for i, (source, target) in enumerate(
+            [(omega_hbm, omega_ref), (pheno_hbm, pheno_ref), (sample_hbm, sample_ref)]
+        )
+    ]
+    for copy in own:
+        copy.start()
     barrier = pltpu.get_barrier_semaphore()
     for partner in partners:
         pl.semaphore_signal(barrier, inc=1, device_id=partner, device_id_type=MESH)
-    acc[...] = jnp.zeros_like(acc)
-    var_acc[...] = jnp.zeros_like(var_acc)
-    own.wait()
+    own[0].wait()
+    own[1].wait()
+    whiten(pheno_ref, omega_ref, size_ref, got.at[0])
     pl.semaphore_wait(barrier, len(partners))
 
     def remote(source, target, send, recv, device):
@@ -215,66 +222,75 @@
                 for j in range(8):
                     flat[pl.ds(base + h * 64 + j, 8, stride=8), :] = value[8 * h : 8 * h + 8, 128 * j : 128 * j + 128]
 
-    def pick_rows(first, last):
-        @pl.loop(first, last)
+    def pick_rows(t):
+        a, b = HOPS_Z[t // NY], HOPS_Y[t % NY]
+        origin = ((z - forward * a + NZ) % NZ) * NY + (y - forward * b + NY) % NY
+        first = origin * B
+
+        @pl.loop(0, B // GROUP)
         def _(g):
-            t = g // (B // GROUP)
-            ia, ib = t // NY, t % NY
-            a = (1 - 2 * ((ia + 1) % 2)) * ((ia + 1) // 2)
-            b = (1 - 2 * ((ib + 1) % 2)) * ((ib + 1) // 2)
-            origin = ((z - forward * a + NZ) % NZ) * NY + (y - forward * b + NY) % NY
-            start = origin * B + (g % (B // GROUP)) * GROUP
+            start = first + g * GROUP
             for q in range(GROUP // 16):
                 rows = jnp.stack([split[sample_ref[start + q * 16 + u]] for u in range(16)], 0)
                 turned = pltpu.einshape("kjl->jkl", rows).astype(jnp.bfloat16)
-                at = pl.multiple_of(g * GROUP + q * 16, 16)
+                at = pl.multiple_of(t * B + g * GROUP + q * 16, 16)
                 for j in range(8):
                     ordered[pl.ds(at, 16), 128 * j : 128 * j + 128] = turned[j]
 
-    def multiply(t):
-        @pl.loop(0, M // 256)
-        def _(n):
-            columns = pl.ds(pl.multiple_of(n * 256, 256), 256)
-            right = ordered[pl.ds(t * B, B), columns]
-            acc[:, columns] += jnp.dot(got[t, :T, :], right, preferred_element_type=jnp.float32)
-            var_acc[:, columns] += jnp.dot(got[t, T:, :], right * right, preferred_element_type=jnp.float32)
+    def multiply(s):
+        left = jnp.concatenate([got[2 * s, :T, :], got[2 * s + 1, :T, :]], axis=1)
+        extra = jnp.concatenate([got[2 * s, T:, :], got[2 * s + 1, T:, :]], axis=1)
+        right = ordered[pl.ds(s * 2 * B, 2 * B), :]
+        acc[...] += jnp.dot(left, right, preferred_element_type=jnp.float32)
+        var_acc[...] += jnp.dot(extra, right * right, preferred_element_type=jnp.float32)
+        scale_acc[...] += extra[:, :B].astype(jnp.float32) + extra[:, B:].astype(jnp.float32)
 
     clock = 0.0
     to_split = list(range(LOADS))
-    picked, groups = 0, NBINS * B // GROUP
+    picked = 0
     seen, ready = {}, []
 
     def work(until):
         nonlocal clock, picked
         while clock < until:
             if to_split:
+                clock = max(clock, LOADED[0] + LOADED[1] * (to_split[0] + 1))
+                if clock >= until:
+                    return
                 split_rows(to_split.pop(0))
                 clock += COST["split"]
-            elif ready and (ready[0] + 1) * (B // GROUP) <= picked:
+            elif ready and (ready[0] + 1) * 2 <= picked:
                 multiply(ready.pop(0))
                 clock += COST["multiply"]
-            elif picked < groups:
-                count = min(B // GROUP, groups - picked)
-                pick_rows(picked, picked + count)
-                picked += count
-                clock += COST["pick"] * count
+            elif picked < NBINS:
+                pick_rows(picked)
+                picked += 1
+                clock += COST["pick"]
             else:
                 return
 
-    for when, p, a, b in GATHER:
+    for n, (when, p, a, b) in enumerate(GATHER):
+        when = max(0.0, when * PACE - LEAD)
         work(when)
         await_and_forward(p, a, b)
-        seen[(a, b)] = seen.get((a, b), 0) + 1
-        if seen[(a, b)] == len(PARTS):
-            ready.append(slot(a, b))
+        clock = max(clock, when) + COST["forward"]
+        pair = slot(a, b) // 2
+        seen[pair] = seen.get(pair, 0) + 1
+        if seen[pair] == 2 * len(PARTS):
+            ready.append(pair)
             ready.sort()
+        if n == len(PARTS) - 1:
+            for load in loads:
+                load.start()
+            acc[...] = jnp.zeros_like(acc)
+            var_acc[...] = jnp.zeros_like(var_acc)
+            scale_acc[...] = jnp.zeros_like(scale_acc)
+            own[2].wait()
     work(float("inf"))
     for copy in sends:
         copy.wait_send()
 
-    scale = got[0, T + 1 : T + 4, :].astype(jnp.float32).sum(axis=0, keepdims=True)
-    for t in range(1, NBINS):
-        scale += got[t, T + 1 : T + 4, :].astype(jnp.float32).sum(axis=0, keepdims=True)
+    scale = scale_acc[1:2, :] + scale_acc[2:3, :] + scale_acc[3:4, :]
     small_out[0, :, :M] = var_acc[0:1, :]
     small_out[0, :, M:] = scale
     smalls = [remote(small_out.at[0], small_in.at[0], small_send.at[0], small_recv.at[0], sibling)]
@@ -321,41 +337,46 @@
     out_ref[...] = total * root
 
 
-def score(samples, message, dosages):
+def score(samples, sizes, phenotype, blocks, dosages):
     vmem = pl.BlockSpec(memory_space=pltpu.VMEM)
-    anywhere = pl.BlockSpec(memory_space=pl.ANY)
+    smem = pl.BlockSpec(memory_space=pltpu.SMEM)
+    hbm = pl.BlockSpec(memory_space=pltpu.HBM)
     dma = pltpu.SemaphoreType.DMA
     n_sends = sum(len(forwards(p, a, b)) for _, p, a, b in GATHER)
     return pl.pallas_call(
         scores_kernel,
         name="scores",
         out_shape=jax.ShapeDtypeStruct((32, M), jnp.float32),
-        in_specs=[pl.BlockSpec(memory_space=pltpu.SMEM), anywhere, anywhere],
+        in_specs=[smem, hbm, hbm, hbm, hbm],
         out_specs=vmem,
         scratch_shapes=[
+            pltpu.SMEM((NBINS * B,), jnp.int32),
+            pltpu.VMEM((B, T), jnp.bfloat16),
+            pltpu.VMEM((1, B, B), jnp.float32),
             pltpu.VMEM((N, 8, 128), jnp.float32),
             pltpu.VMEM((NBINS * B, M), jnp.bfloat16),
             pltpu.VMEM((NBINS, MSG, B), jnp.bfloat16),
             pltpu.VMEM((T, M), jnp.float32),
             pltpu.VMEM((16, M), jnp.float32),
+            pltpu.VMEM((16, T), jnp.float32),
             pltpu.VMEM((4, 32, M), jnp.bfloat16),
             pltpu.VMEM((4, 32, M), jnp.bfloat16),
             pltpu.VMEM((3, 32, M), jnp.bfloat16),
             pltpu.VMEM((3, 32, M), jnp.bfloat16),
             pltpu.VMEM((2, 1, TS), jnp.float32),
             pltpu.VMEM((4, 1, TS), jnp.float32),
-            dma((n_sends,)), dma((2, NBINS)), dma((LOADS,)), dma,
+            dma((n_sends,)), dma((2, NBINS)), dma((LOADS,)), dma((3,)),
             dma((4,)), dma((4,)), dma((3,)), dma((3,)), dma((4,)), dma((4,)),
         ],
         compiler_params=pltpu.CompilerParams(
             collective_id=0, has_side_effects=True, vmem_limit_bytes=58 << 20
         ),
-    )(samples, message, dosages)
+    )(sizes, samples, phenotype, blocks, dosages)
 
 
 def local(phenotype, inverse_blocks, bin_sizes, slot_of, dosages):
-    message, samples = prepare(phenotype, inverse_blocks, bin_sizes, slot_of)
-    return score(samples.reshape(NBINS * B), message, dosages).T
+    samples = invert(slot_of).reshape(NBINS * B)
+    return score(samples, bin_sizes, phenotype, inverse_blocks, dosages).T
 
 
 def solution(mesh):

time: 85 us -> 54.6 us (0.64)
  Pallas kernels: 82.5 us -> 52.2 us
    pallas_call x1, Pallas kernels: 80.1 us -> 50.2 us  [score(): pl.pallas_call(scores_kernel, name='scores', out_shape=jax.ShapeDtypeStru...]
where the time goes in v2:
time: 54.6 us; the launch traced here: 54.4 us
  Pallas kernels  52.2 us (96%)
  local copies, waits for them, and re-layouts  1.57 us (3%)
  between operations  0.66 us (1%)
    pallas_call x1, Pallas kernels, score(): pl.pallas_call(scores_kernel, name='scores', out_shape=jax.ShapeDtypeStru...  50.2 us
    pallas_call x1, Pallas kernels, invert(): pl.pallas_call(invert_kernel, name='invert', out_shape=jax.ShapeDtypeStru...  1.96 us
    unnamed x1, local copies, waits for them, and re-layouts  1.57 us

profile of v2, /device:TPU:1, one launch (start us, length us, event | category | flops | bytes accessed | tf_op | source)
XLA Modules:
  0.0 54.4 jit_solution(3870044051132187108)
XLA Ops:
  0.7 2.0 %invert.1 = s32[64,128]{1,0:T(8,128)} custom-call(s32[1,6144]{1,0:T(1,128)} %bitcast.5), custom_call_target="tpu_custom_call" | custom-call | tf_op jit(solution)/shard_map/invert/pallas_call | solution.py:107
  2.6 50.2 %scores.1 = f32[32,1024]{1,0:T(8,128)} custom-call(s32[1,1]{1,0:T(1,128)S(6)} %copy.7.size_ref, s32[8192]{0:T(1024)} %bitcast.4, bf16[256,256]{1,0:T(8,128)(2,1)} %pheno_hbm.1, f32[1,256,256]{2,1,0:T(8,128)} %omega_hbm.1, bf16[6144,1024]{1,0:T(8,128)(2,1)} %dosage_ref.1), custom_call_target="tpu_custom_call" | custom-call | tf_op jit(solution)/shard_map/scores/pallas_call | solution.py:346
  52.8 1.6 %copy.8 = f32[1024,32]{0,1:T(8,128)} copy(f32[1024,32]{0,1:T(8,128)} %bitcast.3) | data formatting | bytes 262144

commit v3 on v2

--- a/solution.py
+++ b/solution.py
@@ -82,7 +82,7 @@
 LOADS = 24
 ROWS = N // LOADS
 GROUP = 64
-PACE, LEAD = 0.8, 0.0
+PACE, LEAD = 0.87, 0.0
 LOADED = (1.5, 0.3)
 COST = dict(split=0.3, pick=0.3, multiply=0.58, forward=0.05)
 
@@ -92,11 +92,11 @@
     chunk = 1024
     for k in range(N // chunk):
         slots = slot_ref[:, k * chunk : (k + 1) * chunk]
-        high, low = slots // 128, slots % 128
+        high, low = slots >> 7, slots & 127
         at = lax.broadcasted_iota(jnp.int32, (128, chunk), 0)
         sample = lax.broadcasted_iota(jnp.int32, (128, chunk), 1) + k * chunk
-        digit = jnp.where(at < 64, sample // 128, sample % 128).astype(jnp.float32)
-        left = jnp.where(at % 64 == high, digit, 0.0).astype(jnp.bfloat16)
+        digit = jnp.where(at < 64, sample >> 7, sample & 127).astype(jnp.float32)
+        left = jnp.where((at & 63) == high, digit, 0.0).astype(jnp.bfloat16)
         right = jnp.where(at == low, 1.0, 0.0).astype(jnp.bfloat16)
         found += lax.dot_general(left, right, (((1,), (1,)), ((), ())), preferred_element_type=jnp.float32)
     sample_ref[...] = (found[:64] * 128.0 + found[64:]).astype(jnp.int32)
@@ -107,6 +107,7 @@
     return pl.pallas_call(
         invert_kernel,
         name="invert",
+        cost_estimate=pl.CostEstimate(flops=4_000_000_000, bytes_accessed=60_000, transcendentals=0),
         out_shape=jax.ShapeDtypeStruct((64, 128), jnp.int32),
         in_specs=[vmem],
         out_specs=vmem,
@@ -287,9 +288,6 @@
             scale_acc[...] = jnp.zeros_like(scale_acc)
             own[2].wait()
     work(float("inf"))
-    for copy in sends:
-        copy.wait_send()
-
     scale = scale_acc[1:2, :] + scale_acc[2:3, :] + scale_acc[3:4, :]
     small_out[0, :, :M] = var_acc[0:1, :]
     small_out[0, :, M:] = scale
@@ -302,13 +300,6 @@
         half_out[d] = acc[rows, :].astype(jnp.bfloat16)
         halves[d] = remote(half_out.at[d], half_in.at[d], half_send.at[d], half_recv.at[d], sibling)
         halves[d].start()
-
-    smalls[0].wait()
-    small_out[1] = small_out[0] + small_in[0]
-    for d in (1, 2, 3):
-        copy = remote(small_out.at[1], small_in.at[d], small_send.at[d], small_recv.at[d], peers[d])
-        copy.start()
-        smalls.append(copy)
 
     pieces = []
     for d in (2, 1, 3, 0):
@@ -322,6 +313,15 @@
             copy = remote(part_out.at[d - 1], part_in.at[d - 1], part_send.at[d - 1], part_recv.at[d - 1], peers[d])
             copy.start()
             pieces.append(copy)
+        if d == 2:
+            smalls[0].wait()
+            small_out[1] = small_out[0] + small_in[0]
+            for far in (2, 1, 3):
+                copy = remote(small_out.at[1], small_in.at[far], small_send.at[far], small_recv.at[far], peers[far])
+                copy.start()
+                smalls.append(copy)
+    for copy in sends:
+        copy.wait_send()
     for copy in smalls[1:]:
         copy.wait()
     small = small_out[1] + small_in[1] + small_in[2] + small_in[3]
@@ -369,7 +369,7 @@
             dma((4,)), dma((4,)), dma((3,)), dma((3,)), dma((4,)), dma((4,)),
         ],
         compiler_params=pltpu.CompilerParams(
-            collective_id=0, has_side_effects=True, vmem_limit_bytes=58 << 20
+            collective_id=0, has_side_effects=True, vmem_limit_bytes=52 << 20
         ),
     )(sizes, samples, phenotype, blocks, dosages)
 

time: 54.6 us -> 53.6 us (0.982)
  Pallas kernels: 52.2 us -> 51.3 us
    pallas_call x1, Pallas kernels: 50.2 us -> 49.3 us  [score(): pl.pallas_call(scores_kernel, name='scores', out_shape=jax.ShapeDtypeStru...]
    unnamed x1 -> x7, local copies, waits for them, and re-layouts: 1.57 us -> 1.42 us
where the time goes in v3:
time: 53.6 us; the launch traced here: 53.4 us
  Pallas kernels  51.3 us (96%)
  local copies, waits for them, and re-layouts  1.42 us (3%)
  between operations  0.71 us (1%)
    pallas_call x1, Pallas kernels, score(): pl.pallas_call(scores_kernel, name='scores', out_shape=jax.ShapeDtypeStru...  49.3 us
    pallas_call x1, Pallas kernels, invert(): pl.pallas_call(invert_kernel, name='invert', cost_estimate=pl.CostEstimat...  1.95 us
    unnamed x7, local copies, waits for them, and re-layouts  1.42 us

profile of v3, /device:TPU:1, one launch (start us, length us, event | category | flops | bytes accessed | tf_op | source)
XLA Modules:
  0.0 53.4 jit_solution(4133885475071219723)
XLA Ops:
  0.0 0.0 copy-start
  0.0 0.0 copy-start.1
  0.7 2.0 %invert.1 = s32[64,128]{1,0:T(8,128)} custom-call(s32[1,6144]{1,0:T(1,128)} %bitcast.5), custom_call_target="tpu_custom_call" | custom-call | flops 4000000000 | bytes 60000 | tf_op jit(solution)/shard_map/invert/pallas_call | solution.py:107
  2.7 0.0 copy-done
  2.7 0.0 copy-done.1
  2.7 0.0 copy-start.2
  2.7 0.8 %copy-done.2 = s32[64,128]{1,0:T(8,128)S(1)} copy-done((s32[64,128]{1,0:T(8,128)S(1)}, s32[64,128]{1,0:T(8,128)}, u32[]{:S(2)}) %copy-start.2) | copy-done | bytes 32792
  3.4 49.3 %scores.1 = f32[32,1024]{1,0:T(8,128)S(1)} custom-call(s32[1,1]{1,0:T(1,128)S(6)} %copy.7.size_ref, s32[8192]{0:T(1024)S(1)} %bitcast.4, bf16[256,256]{1,0:T(8,128)(2,1)S(1)} %copy-done.1, f32[1,256,256]{2,1,0:T(8,128)S(1)} %copy-done, bf16[6144,1024]{1,0:T(8,128)(2,1)} %dosage_ref.1), custom_call_target="tpu_custom_call" | custom-call | tf_op jit(solution)/shard_map/scores/pallas_call | solution.py:346
  52.7 0.7 %copy.8 = f32[1024,32]{0,1:T(8,128)} copy(f32[1024,32]{0,1:T(8,128)S(1)} %bitcast.3) | data formatting | bytes 262144
Async XLA Ops:
  0.0 2.7 %copy-start = (f32[1,256,256]{2,1,0:T(8,128)S(1)}, f32[1,256,256]{2,1,0:T(8,128)}, u32[]{:S(2)}) copy-start(f32[1,256,256]{2,1,0:T(8,128)} %omega_hbm.1) | copy-start | bytes 786436
  0.0 2.7 %copy-start.1 = (bf16[256,256]{1,0:T(8,128)(2,1)S(1)}, bf16[256,256]{1,0:T(8,128)(2,1)}, u32[]{:S(2)}) copy-start(bf16[256,256]{1,0:T(8,128)(2,1)} %pheno_hbm.1) | copy-start | bytes 393220
  2.7 0.8 %copy-start.2 = (s32[64,128]{1,0:T(8,128)S(1)}, s32[64,128]{1,0:T(8,128)}, u32[]{:S(2)}) copy-start(s32[64,128]{1,0:T(8,128)} %invert.1) | copy-start | bytes 98308

commit v4 on v3

--- a/solution.py
+++ b/solution.py
@@ -81,7 +81,7 @@
 GATHER = gather_order(90.0, 4.0, 75.0)
 LOADS = 24
 ROWS = N // LOADS
-GROUP = 64
+GROUP = 128
 PACE, LEAD = 0.87, 0.0
 LOADED = (1.5, 0.3)
 COST = dict(split=0.3, pick=0.3, multiply=0.58, forward=0.05)

time: 53.6 us -> 53.6 us (level)
  no operation moved by 1% of the time
where the time goes in v4:
time: 53.6 us; the launch traced here: 53.4 us
  Pallas kernels  51.2 us (96%)
  local copies, waits for them, and re-layouts  1.42 us (3%)
  between operations  0.72 us (1%)
    pallas_call x1, Pallas kernels, score(): pl.pallas_call(scores_kernel, name='scores', out_shape=jax.ShapeDtypeStru...  49.3 us
    pallas_call x1, Pallas kernels, invert(): pl.pallas_call(invert_kernel, name='invert', cost_estimate=pl.CostEstimat...  1.95 us
    unnamed x7, local copies, waits for them, and re-layouts  1.42 us

profile of v4, /device:TPU:1, one launch (start us, length us, event | category | flops | bytes accessed | tf_op | source)
XLA Modules:
  0.0 53.4 jit_solution(947646661316240688)
XLA Ops:
  0.0 0.0 copy-start
  0.0 0.0 copy-start.1
  0.7 1.9 %invert.1 = s32[64,128]{1,0:T(8,128)} custom-call(s32[1,6144]{1,0:T(1,128)} %bitcast.5), custom_call_target="tpu_custom_call" | custom-call | flops 4000000000 | bytes 60000 | tf_op jit(solution)/shard_map/invert/pallas_call | solution.py:107
  2.7 0.0 copy-done
  2.7 0.0 copy-done.1
  2.7 0.0 copy-start.2
  2.7 0.8 %copy-done.2 = s32[64,128]{1,0:T(8,128)S(1)} copy-done((s32[64,128]{1,0:T(8,128)S(1)}, s32[64,128]{1,0:T(8,128)}, u32[]{:S(2)}) %copy-start.2) | copy-done | bytes 32792
  3.4 49.3 %scores.1 = f32[32,1024]{1,0:T(8,128)S(1)} custom-call(s32[1,1]{1,0:T(1,128)S(6)} %copy.7.size_ref, s32[8192]{0:T(1024)S(1)} %bitcast.4, bf16[256,256]{1,0:T(8,128)(2,1)S(1)} %copy-done.1, f32[1,256,256]{2,1,0:T(8,128)S(1)} %copy-done, bf16[6144,1024]{1,0:T(8,128)(2,1)} %dosage_ref.1), custom_call_target="tpu_custom_call" | custom-call | tf_op jit(solution)/shard_map/scores/pallas_call | solution.py:346
  52.7 0.7 %copy.8 = f32[1024,32]{0,1:T(8,128)} copy(f32[1024,32]{0,1:T(8,128)S(1)} %bitcast.3) | data formatting | bytes 262144
Async XLA Ops:
  0.0 2.7 %copy-start = (f32[1,256,256]{2,1,0:T(8,128)S(1)}, f32[1,256,256]{2,1,0:T(8,128)}, u32[]{:S(2)}) copy-start(f32[1,256,256]{2,1,0:T(8,128)} %omega_hbm.1) | copy-start | bytes 786436
  0.0 2.7 %copy-start.1 = (bf16[256,256]{1,0:T(8,128)(2,1)S(1)}, bf16[256,256]{1,0:T(8,128)(2,1)}, u32[]{:S(2)}) copy-start(bf16[256,256]{1,0:T(8,128)(2,1)} %pheno_hbm.1) | copy-start | bytes 393220
  2.7 0.8 %copy-start.2 = (s32[64,128]{1,0:T(8,128)S(1)}, s32[64,128]{1,0:T(8,128)}, u32[]{:S(2)}) copy-start(s32[64,128]{1,0:T(8,128)} %invert.1) | copy-start | bytes 98308
